TPU v7x, 512 devices: a whole 4x8x8 slice. The times are simulated.
512 devices in a mesh: pop: 32 (over z, x_lo, core), mp: 16 (over x_hi, y).
Axes of the slice: x: 4 (x_hi: 2, x_lo: 2; x = x_hi * 2 + x_lo), y: 8, z: 8, core: 2. Of those that a mesh axis runs over, the one named last changes fastest.
Arguments:
- prompts: bfloat16 [128, 128, 4096], P('pop'), may hold values from -9 to 9
- gate_weight: bfloat16 [4096, 8192], P('pop', 'mp'), may hold values from -0.09375 to 0.09375
- up_weight: bfloat16 [4096, 8192], P('pop', 'mp'), may hold values from -0.09375 to 0.09375
- reward_head: bfloat16 [8192], P('mp'), may hold values from -0.0625 to 0.0625
- member_seeds: int32 [128], P('pop'), may hold values from 0 to 1073741823
- counters: int32 [128], P('pop'), may hold values from 0 to 65535
- member_ranks: int32 [128], P('pop'), may hold values from 0 to 127, each once
Outputs:
- new_gate: bfloat16 [4096, 8192], P('pop', 'mp')
- new_up: bfloat16 [4096, 8192], P('pop', 'mp')
- scores: float32 [128], P('pop')
All inputs are finite; a program needn't handle non-finite values.
Results may differ from a plain program's by a relative error of at most 0.014.
Values may be sent and summed in bfloat16 or wider, within the bound.
A program may use at most 64 MiB of HBM per device.

v0:
```python
import jax
import jax.numpy as jnp
from jax import lax
from jax.sharding import PartitionSpec as P

sigma_perturb = 0.004
learn_rate = 0.0016


def shift_down(number, amount):
    return lax.shift_right_logical(number, jnp.full_like(number, amount))


def mix_bits(number):
    number = number ^ shift_down(number, 16)
    number = number * 2146121005
    number = number ^ shift_down(number, 15)
    number = number * -2073254261
    return number ^ shift_down(number, 16)


def factor_rows(seed_list, counter_list, slot, positions):
    anchor = mix_bits(
        seed_list * 1103515245 + mix_bits(counter_list * 668265263 + slot * 374761393)
    )
    hashed = mix_bits(anchor[:, None] + positions[None, :] * -1640531535)
    uniform_part = shift_down(hashed, 8).astype(jnp.float32) * (1.0 / 16777216.0)
    return (2.0 * uniform_part - 1.0 + 1.0 / 16777216.0) * 1.7320508075688772


def shards(prompts, gate_weight, up_weight, reward_head, member_seeds, counters, member_ranks):
    members_here, seq_len, width = prompts.shape
    own_rows, own_cols = gate_weight.shape
    pop_index = lax.axis_index("pop")
    mp_index = lax.axis_index("mp")
    row_start = pop_index * own_rows
    column_ids = mp_index * own_cols + jnp.arange(own_cols, dtype=jnp.int32)
    all_seeds, all_counters, all_ranks = (
        lax.all_gather(member_seeds, "pop", axis=0, tiled=True),
        lax.all_gather(counters, "pop", axis=0, tiled=True),
        lax.all_gather(member_ranks, "pop", axis=0, tiled=True),
    )
    members_all = all_seeds.shape[0]
    fitness = (all_ranks.astype(jnp.float32) + 0.5) / members_all - 0.5
    scaling = learn_rate / (members_all * sigma_perturb)
    right_gate = factor_rows(all_seeds, all_counters, 1, column_ids).astype(jnp.bfloat16)
    right_up = factor_rows(all_seeds, all_counters, 3, column_ids).astype(jnp.bfloat16)

    def fresh_rows(weight_rows, first_row, slot, right_factor):
        row_ids = first_row + jnp.arange(weight_rows.shape[0], dtype=jnp.int32)
        left_factor = (
            factor_rows(all_seeds, all_counters, slot, row_ids) * fitness[:, None]
        ).astype(jnp.bfloat16)
        update_term = scaling * jnp.dot(
            left_factor.T, right_factor, preferred_element_type=jnp.float32
        )
        return (weight_rows.astype(jnp.float32) + update_term).astype(jnp.bfloat16)

    new_gate = fresh_rows(gate_weight, row_start, 0, right_gate)
    new_up = fresh_rows(up_weight, row_start, 2, right_up)
    flat_rows = prompts.reshape(members_here * seq_len, width)
    gate_base = jnp.dot(
        flat_rows,
        lax.all_gather(new_gate, "pop", axis=0, tiled=True),
        preferred_element_type=jnp.float32,
    )
    up_base = jnp.dot(
        flat_rows,
        lax.all_gather(new_up, "pop", axis=0, tiled=True),
        preferred_element_type=jnp.float32,
    )
    later = counters + 1
    all_positions = jnp.arange(width, dtype=jnp.int32)
    gate_vec = factor_rows(member_seeds, later, 0, all_positions).astype(jnp.bfloat16)
    gate_col = factor_rows(member_seeds, later, 1, column_ids)
    up_vec = factor_rows(member_seeds, later, 2, all_positions).astype(jnp.bfloat16)
    up_col = factor_rows(member_seeds, later, 3, column_ids)
    gate_proj = jnp.einsum("mld,md->ml", prompts, gate_vec, preferred_element_type=jnp.float32)
    up_proj = jnp.einsum("mld,md->ml", prompts, up_vec, preferred_element_type=jnp.float32)
    gate_value = (
        gate_base.reshape(members_here, seq_len, own_cols)
        + sigma_perturb * gate_proj[:, :, None] * gate_col[:, None, :]
    )
    up_value = (
        up_base.reshape(members_here, seq_len, own_cols)
        + sigma_perturb * up_proj[:, :, None] * up_col[:, None, :]
    )
    hidden = (jax.nn.silu(gate_value) * up_value).astype(jnp.bfloat16)
    partial_reward = jnp.einsum("mlf,f->m", hidden, reward_head, preferred_element_type=jnp.float32)
    summed = lax.psum(partial_reward, "mp")
    all_rewards = lax.all_gather(summed, "pop", axis=0, tiled=True)
    rewards = all_rewards / seq_len
    reward_mean = jnp.mean(rewards)
    reward_var = jnp.mean((rewards - reward_mean) ** 2)
    all_scores = (rewards - reward_mean) / jnp.sqrt(reward_var + 1e-05)
    own_scores = lax.dynamic_slice_in_dim(all_scores, pop_index * members_here, members_here)
    return (new_gate, new_up, own_scores)


def solution(mesh):
    in_specs = (
        P("pop", None, None),
        P("pop", "mp"),
        P("pop", "mp"),
        P("mp"),
        P("pop"),
        P("pop"),
        P("pop"),
    )
    out_specs = (P("pop", "mp"), P("pop", "mp"), P("pop"))
    return jax.shard_map(shards, mesh=mesh, in_specs=in_specs, out_specs=out_specs, check_vma=False)
```

profile of v0, /device:TPU:1, one launch (start us, length us, event | category | flops | bytes accessed | tf_op | source)
XLA Modules:
  0.0 286.7 jit_solution(374049594415008718)
XLA Ops:
  7.2 0.0 all-gather.3.cloned.1.call-start
  7.2 1.3 dynamic-slice
  9.2 0.9 dynamic-update-slice
  10.0 0.8 dynamic-update-slice.1
  10.9 0.8 dynamic-update-slice.2
  11.7 20.1 %all-reduce.4 = (s32[128]{0:T(128)S(1)}, s32[128]{0:T(128)S(1)}, s32[128]{0:T(128)S(1)}) all-reduce(s32[128]{0:T(128)S(1)} %dynamic-update-slice, s32[128]{0:T(128)S(1)} %dynamic-update-slice.1, s32[128]{0:T(128)S(1)} %dynamic-update-slice.2), channel_id=1, replica_groups=mesh['pop'=32,'mp'=16] {'pop'}, use_global_device_ids=true, to_apply=%add | all-reduce | flops 384 | bytes 3072
  31.9 2.0 fusion.2
  33.9 0.0 all-gather.3.cloned.1.call-update
  33.9 0.0 all-gather.5.cloned.1.call-start
  33.9 2.0 fusion.3
  35.9 0.0 all-gather.5.cloned.1.call-update
  35.9 0.7 reshape.142
  36.6 0.0 copy-start
  36.6 0.8 shift-right-logical_xor_fusion.42
  37.4 0.2 fusion.80
  37.7 3.6 %fusion.72 = f32[4,1,128]{2,1,0:T(1,128)S(1)} fusion(bf16[4,128,4096]{2,1,0:T(8,128)(2,1)} %param.7, bf16[4,4096,1]{1,0,2:T(4,128)(2,1)S(1)} %get-tuple-element.7), kind=kOutput, calls=%fused_computation.93 | convolution fusion | flops 4194304 | bytes 4229120 | tf_op jit(solution)/shard_map/mld,md->ml/dot_general | solution.py:79
  41.2 0.0 copy-done
  41.2 1.2 fusion.74
  42.5 0.1 fusion.108
  42.6 61.3 %all-gather.3.cloned.1.call-done = bf16[4096,512]{1,0:T(8,128)(2,1)} async-done(((bf16[128,512]{1,0:T(8,128)(2,1)}), bf16[4096,512]{1,0:T(8,128)(2,1)}) %all-gather.3.cloned.1.call-update) | async-done | bytes 4194320 | tf_op jit(solution)/shard_map/all_gather | solution.py:64
  103.9 5.8 %fusion.173 = f32[512,512]{0,1:T(8,128)S(1)} fusion(bf16[512,4096]{1,0:T(8,128)(2,1)} %bitcast.28, bf16[4096,512]{1,0:T(8,128)(2,1)} %all-gather.3.cloned.1.call-done), kind=kOutput, calls=%fused_computation.259 | convolution fusion | flops 2147483648 | bytes 9437184 | tf_op jit(solution)/shard_map/dot_general | solution.py:62
  109.7 66.5 %all-gather.5.cloned.1.call-done = bf16[4096,512]{1,0:T(8,128)(2,1)} async-done(((bf16[128,512]{1,0:T(8,128)(2,1)}), bf16[4096,512]{1,0:T(8,128)(2,1)}) %all-gather.5.cloned.1.call-update) | async-done | bytes 4194320 | tf_op jit(solution)/shard_map/all_gather | solution.py:69
  176.2 6.0 %convert_reduce_fusion = bf16[4,512]{1,0:T(4,128)(2,1)S(1)} fusion(f32[4,512]{1,0:T(4,128)S(1)} %get-tuple-element.9, f32[4,128]{1,0:T(4,128)S(1)} %get-tuple-element.18, f32[4,512]{1,0:T(4,128)S(1)} %get-tuple-element.8, f32[4,128]{1,0:T(4,128)S(1)} %get-tuple-element.19, f32[512,512]{0,1:T(8,128)S(1)} %fusion.173, bf16[512,4096]{1,0:T(8,128)(2,1)} %bitcast.29, ...), kind=kOutput, calls=%fused_computation.7 | convolution fusion | flops 2150627328 | bytes 9461760 | tf_op jit(solution)/shard_map/dot_general | solution.py:67
  182.1 0.1 convolution_bitcast_fusion
  182.3 34.3 %psum.7 = f32[4]{0:T(128)S(1)} all-reduce(f32[4]{0:T(128)S(1)} %convolution_bitcast_fusion), channel_id=1, replica_groups=mesh['pop'=32,'mp'=16] {'mp'}, use_global_device_ids=true, to_apply=%region_1.2 | all-reduce | flops 4 | bytes 32 | tf_op jit(solution)/shard_map/psum | solution.py:90
  216.6 0.2 dynamic-update-slice.3
  216.8 59.9 %all-reduce.3 = f32[128]{0:T(128)S(1)} all-reduce(f32[128]{0:T(128)S(1)} %dynamic-update-slice.3), channel_id=1, replica_groups=mesh['pop'=32,'mp'=16] {'pop'}, use_global_device_ids=true, to_apply=%add.3 | all-reduce | flops 128 | bytes 1024
  276.7 0.6 fusion.156
  277.9 0.6 multiply_reduce_fusion
  279.2 0.6 dynamic_slice.3
  (11 shorter events, 0.1 us)
Async XLA Ops:
  7.2 96.7 %all-gather.3.cloned.1.call-start = ((), (), s32[]{:S(2)}) async-start(), calls=%async_computation | async-start | bytes 4325376 | tf_op jit(solution)/shard_map/all_gather | solution.py:64
  33.9 142.3 %all-gather.5.cloned.1.call-start = ((), (), s32[]{:S(2)}) async-start(), calls=%async_computation.1 | async-start | bytes 4325376 | tf_op jit(solution)/shard_map/all_gather | solution.py:69
  36.6 4.7 %copy-start = (bf16[4,128,4096]{2,1,0:T(8,128)(2,1)S(1)}, bf16[4,128,4096]{2,1,0:T(8,128)(2,1)}, u32[]{:S(2)}) copy-start(bf16[4,128,4096]{2,1,0:T(8,128)(2,1)} %param.7) | copy-start | bytes 12582916
Sparse Core Ops, SparseCore 0:
  34.0 69.8 all-gather.2
  106.6 69.5 all-gather.4
where the time goes:
time: 287 us
  waiting for transfers between devices  128 us (45%)
  blocking collectives  114 us (40%)
  matrix products  20.6 us (7%)
  between operations  16.1 us (6%)
  local copies, waits for them, and re-layouts  5.32 us (2%)
    unnamed x2, blocking collectives  80 us
    all_gather x1, waiting for transfers between devices, shards(): lax.all_gather(new_up, 'pop', axis=0, tiled=True)  66.5 us
    all_gather x1, waiting for transfers between devices, shards(): lax.all_gather(new_gate, 'pop', axis=0, tiled=True)  61.3 us
    psum x1, blocking collectives, shards(): summed = lax.psum(partial_reward, 'mp')  34.3 us
    dot_general x1, matrix products, shards(): jnp.dot(flat_rows, lax.all_gather(new_up, 'pop', axis=0, tiled=True), pre...  5.99 us
    dot_general x1, matrix products, shards(): jnp.dot(flat_rows, lax.all_gather(new_gate, 'pop', axis=0, tiled=True), p...  5.79 us
  transfers between devices with their start and end apart: 2, of which 2 were waited for; matrix products, arithmetic and copies ran while one was open for 5% of the time, Pallas kernels for 0%

commit v1 on v0

--- a/solution.py
+++ b/solution.py
@@ -61,7 +61,15 @@
     flat_rows = prompts.reshape(members_here * seq_len, width)
     gate_base = jnp.dot(
         flat_rows,
-        lax.all_gather(new_gate, "pop", axis=0, tiled=True),
+        jnp.concatenate(
+            lax.all_to_all(
+                jnp.stack([new_gate] * lax.axis_size("pop"), 0),
+                axis_name="pop",
+                split_axis=0,
+                concat_axis=0,
+            ),
+            0,
+        ),
         preferred_element_type=jnp.float32,
     )
     up_base = jnp.dot(

time: 287 us -> 279 us (0.972)
  waiting for transfers between devices: 128 us -> 111 us
  starting transfers between devices: 0.08 us -> 8.57 us
    all_to_all x0 -> x1, waiting for transfers between devices: none -> 111 us  [shards(): lax.all_to_all(jnp.stack([new_gate] * lax.axis_size('pop'), 0), axis_name...]
    all_gather x1, waiting for transfers between devices: 66.5 us -> 0.02 us  [shards(): lax.all_gather(new_up, 'pop', axis=0, tiled=True)]
    all_gather x1 -> x0, waiting for transfers between devices: 61.3 us -> none  [shards(): lax.all_gather(new_gate, 'pop', axis=0, tiled=True)]
    all_to_all x0 -> x1, starting transfers between devices: none -> 8.53 us  [shards(): lax.all_to_all(jnp.stack([new_gate] * lax.axis_size('pop'), 0), axis_name...]
  transfers between devices with their start and end apart: 2 -> 2, of which waited for: 2 -> 1; matrix products, arithmetic and copies ran while one was open for 5% -> 4% of each run, Pallas kernels for 0% -> 0%
where the time goes in v1:
time: 279 us
  blocking collectives  115 us (41%)
  waiting for transfers between devices  111 us (40%)
  matrix products  19 us (7%)
  between operations  16.2 us (6%)
  starting transfers between devices  8.57 us (3%)
  local copies, waits for them, and re-layouts  7.11 us (3%)
    all_to_all x1, waiting for transfers between devices, shards(): lax.all_to_all(jnp.stack([new_gate] * lax.axis_size('pop'), 0), axis_name...  111 us
    unnamed x2, blocking collectives  80.2 us
    psum x1, blocking collectives, shards(): summed = lax.psum(partial_reward, 'mp')  35 us
    all_to_all x1, starting transfers between devices, shards(): lax.all_to_all(jnp.stack([new_gate] * lax.axis_size('pop'), 0), axis_name...  8.53 us
    dot_general x1, matrix products, shards(): jnp.dot(flat_rows, lax.all_gather(new_up, 'pop', axis=0, tiled=True), pre...  5.99 us
    dot_general x1, matrix products, shards(): jnp.dot(flat_rows, jnp.concatenate(lax.all_to_all(jnp.stack([new_gate] *...  5.79 us
  transfers between devices with their start and end apart: 2, of which 1 were waited for; matrix products, arithmetic and copies ran while one was open for 4% of the time, Pallas kernels for 0%

profile of v1, /device:TPU:1, one launch (start us, length us, event | category | flops | bytes accessed | tf_op | source)
XLA Modules:
  0.0 279.1 jit_solution(9262275239745429642)
XLA Ops:
  7.2 1.3 dynamic-slice
  9.1 0.9 dynamic-update-slice
  10.0 0.8 dynamic-update-slice.1
  10.8 0.8 dynamic-update-slice.2
  11.6 20.1 %all-reduce.4 = (s32[128]{0:T(128)S(1)}, s32[128]{0:T(128)S(1)}, s32[128]{0:T(128)S(1)}) all-reduce(s32[128]{0:T(128)S(1)} %dynamic-update-slice, s32[128]{0:T(128)S(1)} %dynamic-update-slice.1, s32[128]{0:T(128)S(1)} %dynamic-update-slice.2), channel_id=1, replica_groups=mesh['pop'=32,'mp'=16] {'pop'}, use_global_device_ids=true, to_apply=%add | all-reduce | flops 384 | bytes 3072
  31.8 1.3 fusion.2
  33.2 0.0 copy-start.1
  33.2 2.4 stack.2
  35.6 0.0 copy-done.1
  35.6 8.5 %all-to-all-start = ((bf16[32,128,512]{2,1,0:T(8,128)(2,1)}), bf16[32,128,512]{2,1,0:T(8,128)(2,1)}, u32[]{:S(2)}, u32[]{:S(2)}) async-start(bf16[32,128,512]{2,1,0:T(8,128)(2,1)} %stack.2), calls=%async_computation | async-start | bytes 8388608 | tf_op jit(solution)/shard_map/all_to_all | solution.py:65
  44.2 0.0 all-gather.2.cloned.1.call-start
  44.2 0.0 copy-done.5
  44.2 1.1 fusion.3
  45.3 0.0 all-gather.2.cloned.1.call-update
  45.3 0.0 copy-done.2
  45.3 0.0 copy-start
  45.4 0.0 copy-done.3
  45.4 0.2 fusion.80
  45.6 3.5 %fusion.72 = f32[4,1,128]{2,1,0:T(1,128)S(1)} fusion(bf16[4,128,4096]{2,1,0:T(8,128)(2,1)} %param.7, bf16[4,4096,1]{1,0,2:T(4,128)(2,1)S(1)} %get-tuple-element.7), kind=kOutput, calls=%fused_computation.93 | convolution fusion | flops 4194304 | bytes 4229120 | tf_op jit(solution)/shard_map/mld,md->ml/dot_general | solution.py:87
  49.1 1.2 fusion.74
  50.3 0.1 fusion.108
  50.4 111.4 %all-to-all-done = bf16[32,128,512]{2,1,0:T(8,128)(2,1)} async-done(((bf16[32,128,512]{2,1,0:T(8,128)(2,1)}), bf16[32,128,512]{2,1,0:T(8,128)(2,1)}, u32[]{:S(2)}, u32[]{:S(2)}) %all-to-all-start) | async-done | bytes 4194336 | tf_op jit(solution)/shard_map/all_to_all | solution.py:65
  161.9 5.8 %fusion.173 = f32[512,512]{0,1:T(8,128)S(1)} fusion(bf16[512,4096]{1,0:T(8,128)(2,1)} %bitcast.29, bf16[4096,512]{1,0:T(8,128)(2,1)} %bitcast.1), kind=kOutput, calls=%fused_computation.259 | convolution fusion | flops 2147483648 | bytes 9437184 | tf_op jit(solution)/shard_map/dot_general | solution.py:62
  167.7 0.0 all-gather.2.cloned.1.call-done
  167.7 6.0 %convert_reduce_fusion = bf16[4,512]{1,0:T(4,128)(2,1)S(1)} fusion(f32[4,512]{1,0:T(4,128)S(1)} %get-tuple-element.9, f32[4,128]{1,0:T(4,128)S(1)} %get-tuple-element.18, f32[4,512]{1,0:T(4,128)S(1)} %get-tuple-element.8, f32[4,128]{1,0:T(4,128)S(1)} %get-tuple-element.19, f32[512,512]{0,1:T(8,128)S(1)} %fusion.173, bf16[512,4096]{1,0:T(8,128)(2,1)} %bitcast.30, ...), kind=kOutput, calls=%fused_computation.7 | convolution fusion | flops 2150627328 | bytes 9461760 | tf_op jit(solution)/shard_map/dot_general | solution.py:75
  173.7 0.1 convolution_bitcast_fusion
  173.8 35.0 %psum.7 = f32[4]{0:T(128)S(1)} all-reduce(f32[4]{0:T(128)S(1)} %convolution_bitcast_fusion), channel_id=1, replica_groups=mesh['pop'=32,'mp'=16] {'mp'}, use_global_device_ids=true, to_apply=%region_1.2 | all-reduce | flops 4 | bytes 32 | tf_op jit(solution)/shard_map/psum | solution.py:98
  208.8 0.2 dynamic-update-slice.3
  209.0 60.0 %all-reduce.3 = f32[128]{0:T(128)S(1)} all-reduce(f32[128]{0:T(128)S(1)} %dynamic-update-slice.3), channel_id=1, replica_groups=mesh['pop'=32,'mp'=16] {'pop'}, use_global_device_ids=true, to_apply=%add.3 | all-reduce | flops 128 | bytes 1024
  269.1 0.6 fusion.156
  270.3 0.6 multiply_reduce_fusion
  271.6 0.6 dynamic_slice.3
  (19 shorter events, 0.1 us)
Async XLA Ops:
  33.2 2.5 copy-start.1
  35.6 8.6 %copy-start.5 = (bf16[128,512]{1,0:T(8,128)(2,1)S(1)}, bf16[128,512]{1,0:T(8,128)(2,1)}, u32[]{:S(2)}) copy-start(bf16[128,512]{1,0:T(8,128)(2,1)} %param.9) | copy-start | bytes 393220
  35.6 9.7 %copy-start.2 = (bf16[512]{0:T(512)(128)(2,1)S(1)}, bf16[512]{0:T(512)(128)(2,1)}, u32[]{:S(2)}) copy-start(bf16[512]{0:T(512)(128)(2,1)} %param.10) | copy-start | bytes 3076
  35.6 9.7 %copy-start.3 = (s32[4]{0:T(128)S(1)}, s32[4]{0:T(128)}, u32[]{:S(2)}) copy-start(s32[4]{0:T(128)} %param.11) | copy-start | bytes 52
  35.6 9.7 %copy-start.4 = (s32[4]{0:T(128)S(1)}, s32[4]{0:T(128)}, u32[]{:S(2)}) copy-start(s32[4]{0:T(128)} %param.12) | copy-start | bytes 52
  35.6 126.2 %all-to-all-start = ((bf16[32,128,512]{2,1,0:T(8,128)(2,1)}), bf16[32,128,512]{2,1,0:T(8,128)(2,1)}, u32[]{:S(2)}, u32[]{:S(2)}) async-start(bf16[32,128,512]{2,1,0:T(8,128)(2,1)} %stack.2), calls=%async_computation | async-start | bytes 8388608 | tf_op jit(solution)/shard_map/all_to_all | solution.py:65
  44.2 123.5 %all-gather.2.cloned.1.call-start = ((), (), s32[]{:S(2)}) async-start(), calls=%async_computation.1 | async-start | bytes 4325376 | tf_op jit(solution)/shard_map/all_gather | solution.py:77
  45.3 3.8 %copy-start = (bf16[4,128,4096]{2,1,0:T(8,128)(2,1)S(1)}, bf16[4,128,4096]{2,1,0:T(8,128)(2,1)}, u32[]{:S(2)}) copy-start(bf16[4,128,4096]{2,1,0:T(8,128)(2,1)} %param.7) | copy-start | bytes 12582916
Sparse Core Ops, SparseCore 0:
  47.7 109.4 all-gather.1
